TPU v7x, 128 devices: a whole 4x4x4 slice. The times are simulated.
128 devices in a mesh: grp: 8 (over y, z_lo), tp: 16 (over z_hi, x, core).
Axes of the slice: x: 4, y: 4, z: 4 (z_hi: 2, z_lo: 2; z = z_hi * 2 + z_lo), core: 2. Of those that a mesh axis runs over, the one named last changes fastest.
Arguments:
- features: bfloat16 [2048, 49152], P('grp', 'tp'), may hold values from -24 to 24
- weight: bfloat16 [49152, 8192], P('tp', 'grp'), may hold values from -0.049804688 to 0.049804688
- norm_gain: float32 [8192], P('grp'), may hold values from 0.1 to 1.9
- target: bfloat16 [2048, 8192], P(None, 'grp'), may hold values from -6 to 6
- counts: int32 [256], replicated, may hold values from 1 to 8
Outputs:
- weight_grad: bfloat16 [49152, 8192], P('tp', 'grp')
- draft_loss: float32 [], replicated
All inputs are finite; a program needn't handle non-finite values.
Results may differ from a plain program's by a relative error of at most 0.0085.
Values may be sent and summed in bfloat16 or wider, within the bound.
A program may use at most 128 MiB of HBM per device.

v0:
```python
import jax
import jax.numpy as jnp
from jax import lax
from jax.sharding import PartitionSpec as P

DOUT = 8192
SPEC = 8
epsilon = 1e-06


def row_mask(counts, row_start, row_count):
    row_index = row_start + jnp.arange(row_count, dtype=jnp.int32)
    owner = jnp.take(counts, row_index // SPEC)
    return (row_index % SPEC < owner).astype(jnp.float32)[:, None]


def backward_rows(hidden, target_rows, row_live, norm_gain, accepted):
    gain_row = norm_gain[None, :]
    squares = lax.psum(jnp.sum(hidden * hidden, axis=1), "grp")
    inverse_rms = lax.rsqrt(squares / DOUT + epsilon)[:, None]
    normed = hidden * inverse_rms * gain_row
    deviation = normed - target_rows
    residual = row_live * deviation / accepted
    coupling = lax.psum(jnp.sum(gain_row * residual * hidden, axis=1), "grp")[:, None]
    act_grad = (
        inverse_rms * gain_row * residual - hidden * inverse_rms**3 * coupling / DOUT
    ).astype(jnp.bfloat16)
    partial_loss = 0.5 * jnp.sum(residual * deviation)
    return (act_grad, partial_loss)


def shards(features, weight, norm_gain, target, counts):
    gathered = lax.all_gather(features, "grp", axis=0, tiled=True)
    total_rows = gathered.shape[0]
    accepted = jnp.sum(counts).astype(jnp.float32)
    rows_here = total_rows // lax.axis_size("tp")
    row_start = lax.axis_index("tp") * rows_here
    hidden = lax.psum_scatter(
        jnp.dot(gathered, weight, preferred_element_type=jnp.float32).astype(jnp.bfloat16),
        "tp",
        scatter_dimension=0,
        tiled=True,
    ).astype(jnp.float32)
    target_rows = lax.dynamic_slice_in_dim(target, row_start, rows_here, 0).astype(jnp.float32)
    row_live = row_mask(counts, row_start, rows_here)
    act_grad, partial_loss = backward_rows(hidden, target_rows, row_live, norm_gain, accepted)
    all_grad = lax.all_gather(act_grad, "tp", axis=0, tiled=True)
    draft_loss = lax.psum(partial_loss, ("grp", "tp"))
    weight_grad = lax.dot_general(
        gathered, all_grad, (((0,), (0,)), ((), ())), preferred_element_type=jnp.float32
    ).astype(jnp.bfloat16)
    return (weight_grad, draft_loss)


def solution(mesh):
    placed = (P("grp", "tp"), P("tp", "grp"), P("grp"), P(None, "grp"), P())
    return jax.shard_map(
        shards, mesh=mesh, in_specs=placed, out_specs=(P("tp", "grp"), P()), check_vma=False
    )
```

profile of v0, /device:TPU:1, one launch (start us, length us, event | category | flops | bytes accessed | tf_op | source)
XLA Modules:
  0.0 507.1 jit_solution(5090543502613461760)
XLA Ops:
  7.2 0.0 all-gather.3.cloned.1.call-start
  7.2 0.7 all-gather.3.cloned.1.call-update
  7.9 0.0 copy-start
  7.9 0.0 copy-start.1
  7.9 0.0 reduce-scatter.2.cloned.1.call-start
  8.0 251.7 %all-gather.3.cloned.1.call-done = bf16[2048,3072]{1,0:T(8,128)(2,1)} async-done(((bf16[256,3072]{1,0:T(8,128)(2,1)}), bf16[2048,3072]{1,0:T(8,128)(2,1)}) %all-gather.3.cloned.1.call-update) | async-done | bytes 12582928 | tf_op jit(solution)/shard_map/all_gather | solution.py:33
  259.7 18.8 %convolution_convert_fusion = bf16[2048,1024]{1,0:T(8,128)(2,1)} fusion(bf16[2048,3072]{1,0:T(8,128)(2,1)} %all-gather.3.cloned.1.call-done, bf16[3072,1024]{1,0:T(8,128)(2,1)} %param.6), kind=kOutput, calls=%fused_computation.2 | convolution fusion | flops 12886999040 | bytes 23068672 | tf_op jit(solution)/shard_map/dot_general | solution.py:39
  278.5 0.0 reduce-scatter.2.cloned.1.call-update
  278.5 0.0 all-gather.5.cloned.1.call-start
  278.5 0.0 copy-done
  278.5 0.6 reduce_sum.37
  279.9 1.3 gather_fusion
  281.2 77.8 %reduce-scatter.2.cloned.1.call-done = bf16[128,1024]{1,0:T(8,128)(2,1)} async-done(((bf16[2048,1024]{1,0:T(8,128)(2,1)}), bf16[128,1024]{1,0:T(8,128)(2,1)}) %reduce-scatter.2.cloned.1.call-update) | async-done | bytes 262160 | tf_op jit(solution)/shard_map/reduce_scatter | solution.py:38
  359.0 1.1 fusion
  360.1 15.3 %psum.21 = f32[128]{0:T(128)S(1)} all-reduce(f32[128]{0:T(128)S(1)} %fusion), channel_id=1, replica_groups=mesh['grp'=8,'tp'=16] {'grp'}, use_global_device_ids=true, to_apply=%region_2.3 | all-reduce | flops 128 | bytes 1024 | tf_op jit(solution)/shard_map/psum | solution.py:19
  375.4 0.0 copy-done.1
  375.4 2.0 multiply_reduce_fusion
  377.4 12.5 %psum.22 = f32[128]{0:T(128)S(1)} all-reduce(f32[128]{0:T(128)S(1)} %get-tuple-element.7), channel_id=1, replica_groups=mesh['grp'=8,'tp'=16] {'grp'}, use_global_device_ids=true, to_apply=%region_5.6 | all-reduce | flops 128 | bytes 1024 | tf_op jit(solution)/shard_map/psum | solution.py:24
  389.9 2.0 fusion.6
  391.9 0.0 all-gather.5.cloned.1.call-update
  392.6 80.8 %psum.23 = f32[]{:T(128)} all-reduce(f32[]{:T(128)S(6)} %mul_shard_map.3), channel_id=1, replica_groups=mesh['grp'=8,'tp'=16] {'grp','tp'}, use_global_device_ids=true, to_apply=%region_7.8 | all-reduce | flops 1 | bytes 8 | tf_op jit(solution)/shard_map/psum | solution.py:48
  473.4 0.0 all-gather.5.cloned.1.call-done
  473.4 18.6 %convert_bitcast_fusion = bf16[3072,1024]{0,1:T(8,128)(2,1)} fusion(bf16[2048,1024]{1,0:T(8,128)(2,1)} %all-gather.5.cloned.1.call-done, bf16[2048,3072]{1,0:T(8,128)(2,1)} %all-gather.3.cloned.1.call-done), kind=kOutput, calls=%fused_computation.1 | convolution fusion | flops 12888047616 | bytes 23068672 | tf_op jit(solution)/shard_map/dot_general | solution.py:49
  492.0 8.6 %copy.8 = bf16[3072,1024]{1,0:T(8,128)(2,1)} copy(bf16[3072,1024]{0,1:T(8,128)(2,1)} %convert_bitcast_fusion) | data formatting | bytes 12582912
  (4 shorter events, 0.0 us)
Async XLA Ops:
  7.2 252.5 %all-gather.3.cloned.1.call-start = ((), (), s32[]{:S(2)}) async-start(), calls=%async_computation.1 | async-start | bytes 14155776 | tf_op jit(solution)/shard_map/all_gather | solution.py:33
  7.9 270.6 %copy-start = (s32[256]{0:T(256)S(1)}, s32[256]{0:T(256)}, u32[]{:S(2)}) copy-start(s32[256]{0:T(256)} %param.9) | copy-start | bytes 3076
  7.9 367.5 %copy-start.1 = (f32[1024]{0:T(1024)S(1)}, f32[1024]{0:T(1024)}, u32[]{:S(2)}) copy-start(f32[1024]{0:T(1024)} %param.7) | copy-start | bytes 12292
  7.9 351.1 %reduce-scatter.2.cloned.1.call-start = ((), (), s32[]{:S(2)}) async-start(), calls=%async_computation.2 | async-start | bytes 4456448 | tf_op jit(solution)/shard_map/reduce_scatter | solution.py:38
  278.5 194.9 %all-gather.5.cloned.1.call-start = ((), (), s32[]{:S(2)}) async-start(), calls=%async_computation.3 | async-start | bytes 4456448 | tf_op jit(solution)/shard_map/all_gather | solution.py:47
Sparse Core Ops, SparseCore 0:
  9.6 250.0 all-gather.2
  278.6 80.3 reduce-scatter.1
  392.1 62.8 all-gather.4
where the time goes:
time: 508 us; the launch traced here: 507 us
  waiting for transfers between devices  330 us (65%)
  blocking collectives  109 us (21%)
  matrix products  37.4 us (7%)
  between operations  15.1 us (3%)
  local copies, waits for them, and re-layouts  9.89 us (2%)
  other arithmetic  5.84 us (1%)
    all_gather x1, waiting for transfers between devices, shards(): gathered = lax.all_gather(features, 'grp', axis=0, tiled=True)  252 us
    psum x1, blocking collectives, shards(): draft_loss = lax.psum(partial_loss, ('grp', 'tp'))  80.8 us
    reduce_scatter x1, waiting for transfers between devices, shards(): lax.psum_scatter(jnp.dot(gathered, weight, preferred_element_type=jnp.flo...  77.8 us
    dot_general x1, matrix products, shards(): jnp.dot(gathered, weight, preferred_element_type=jnp.float32)  18.8 us
    dot_general x1, matrix products, shards(): lax.dot_general(gathered, all_grad, (((0,), (0,)), ((), ())), preferred_e...  18.6 us
    psum x1, blocking collectives, backward_rows(): squares = lax.psum(jnp.sum(hidden * hidden, axis=1), 'grp')  15.3 us
    psum x1, blocking collectives, backward_rows(): lax.psum(jnp.sum(gain_row * residual * hidden, axis=1), 'grp')[:, None]  12.5 us
  transfers between devices with their start and end apart: 3, of which 2 were waited for; matrix products, arithmetic and copies ran while one was open for 0% of the time, Pallas kernels for 0%

commit v1 on v0

--- a/solution.py
+++ b/solution.py
@@ -30,7 +30,9 @@
 
 
 def shards(features, weight, norm_gain, target, counts):
-    gathered = lax.all_gather(features, "grp", axis=0, tiled=True)
+    gathered = jnp.concatenate(
+        lax.all_to_all(jnp.stack([features] * lax.axis_size("grp")), "grp", 0, 0), axis=0
+    )
     total_rows = gathered.shape[0]
     accepted = jnp.sum(counts).astype(jnp.float32)
     rows_here = total_rows // lax.axis_size("tp")

time: 508 us -> 411 us (0.81)
  waiting for transfers between devices: 330 us -> 78.4 us
  blocking collectives: 109 us -> 255 us
  local copies, waits for them, and re-layouts: 9.89 us -> 22 us
    all_gather x1 -> x0, waiting for transfers between devices: 252 us -> none  [shards(): gathered = lax.all_gather(features, 'grp', axis=0, tiled=True)]
    all_to_all x0 -> x1, blocking collectives: none -> 146 us  [shards(): lax.all_to_all(jnp.stack([features] * lax.axis_size('grp')), 'grp', 0, 0)]
    another operation x0 -> x1, local copies, waits for them, and re-layouts: none -> 7.58 us  [shards(): jnp.stack([features] * lax.axis_size('grp'))]
    unnamed x5 -> x9, local copies, waits for them, and re-layouts: 8.62 us -> 13.2 us
  transfers between devices with their start and end apart: 3 -> 2, of which waited for: 2 -> 1; matrix products, arithmetic and copies ran while one was open for 0% -> 0% of each run, Pallas kernels for 0% -> 0%
where the time goes in v1:
time: 411 us; the launch traced here: 410 us
  blocking collectives  255 us (62%)
  waiting for transfers between devices  78.4 us (19%)
  matrix products  33.4 us (8%)
  local copies, waits for them, and re-layouts  22 us (5%)
  between operations  15.4 us (4%)
  other arithmetic  5.84 us (1%)
    all_to_all x1, blocking collectives, shards(): lax.all_to_all(jnp.stack([features] * lax.axis_size('grp')), 'grp', 0, 0)  146 us
    psum x1, blocking collectives, shards(): draft_loss = lax.psum(partial_loss, ('grp', 'tp'))  80.7 us
    reduce_scatter x1, waiting for transfers between devices, shards(): lax.psum_scatter(jnp.dot(gathered, weight, preferred_element_type=jnp.flo...  78.4 us
    dot_general x1, matrix products, shards(): lax.dot_general(gathered, all_grad, (((0,), (0,)), ((), ())), preferred_e...  18.6 us
    psum x1, blocking collectives, backward_rows(): squares = lax.psum(jnp.sum(hidden * hidden, axis=1), 'grp')  15.3 us
    dot_general x1, matrix products, shards(): jnp.dot(gathered, weight, preferred_element_type=jnp.float32)  14.8 us
    unnamed x9, local copies, waits for them, and re-layouts  13.2 us
    psum x1, blocking collectives, backward_rows(): lax.psum(jnp.sum(gain_row * residual * hidden, axis=1), 'grp')[:, None]  12.5 us
  transfers between devices with their start and end apart: 2, of which 1 were waited for; matrix products, arithmetic and copies ran while one was open for 0% of the time, Pallas kernels for 0%

profile of v1, /device:TPU:1, one launch (start us, length us, event | category | flops | bytes accessed | tf_op | source)
XLA Modules:
  0.0 410.1 jit_solution(1600271808743552085)
XLA Ops:
  7.2 0.0 reduce-scatter.2.cloned.1.call-start
  7.2 7.6 %stack.2 = bf16[8,256,3072]{2,1,0:T(8,128)(2,1)} broadcast(bf16[256,3072]{1,0:T(8,128)(2,1)} %param.5), dimensions={1,2} | broadcast | bytes 14155776 | tf_op jit(solution)/shard_map/stack | solution.py:34
  14.8 0.0 copy-start.3
  14.8 146.4 %all_to_all.5 = bf16[8,256,3072]{2,1,0:T(8,128)(2,1)S(1)} all-to-all(bf16[8,256,3072]{2,1,0:T(8,128)(2,1)} %stack.2), channel_id=1, replica_groups=mesh['grp'=8,'tp'=16] {'grp'}, dimensions={0} | all-to-all | bytes 25165824 | tf_op jit(solution)/shard_map/all_to_all | solution.py:34
  161.2 0.0 copy-start.1
  161.2 4.6 %copy-done.1 = bf16[8,256,3072]{2,1,0:T(8,128)(2,1)} copy-done((bf16[8,256,3072]{2,1,0:T(8,128)(2,1)}, bf16[8,256,3072]{2,1,0:T(8,128)(2,1)S(1)}, u32[]{:S(2)}) %copy-start.1) | copy-done | bytes 12582936
  165.8 0.0 copy-done.3
  165.8 0.0 copy-start
  165.8 0.0 copy-start.2
  165.8 14.8 %convolution_convert_fusion = bf16[2048,1024]{1,0:T(8,128)(2,1)} fusion(bf16[2048,3072]{1,0:T(8,128)(2,1)S(1)} %bitcast.9, bf16[3072,1024]{1,0:T(8,128)(2,1)S(1)} %copy-done.3), kind=kOutput, calls=%fused_computation.2 | convolution fusion | flops 12886999040 | bytes 23068672 | tf_op jit(solution)/shard_map/dot_general | solution.py:41
  180.5 0.0 reduce-scatter.2.cloned.1.call-update
  180.6 0.0 all-gather.2.cloned.1.call-start
  180.6 0.0 copy-done
  180.6 0.6 reduce_sum.37
  181.9 1.3 gather_fusion
  183.2 78.4 %reduce-scatter.2.cloned.1.call-done = bf16[128,1024]{1,0:T(8,128)(2,1)} async-done(((bf16[2048,1024]{1,0:T(8,128)(2,1)}), bf16[128,1024]{1,0:T(8,128)(2,1)}) %reduce-scatter.2.cloned.1.call-update) | async-done | bytes 262160 | tf_op jit(solution)/shard_map/reduce_scatter | solution.py:40
  261.6 1.1 fusion
  262.7 15.3 %psum.21 = f32[128]{0:T(128)S(1)} all-reduce(f32[128]{0:T(128)S(1)} %fusion), channel_id=1, replica_groups=mesh['grp'=8,'tp'=16] {'grp'}, use_global_device_ids=true, to_apply=%region_2.3 | all-reduce | flops 128 | bytes 1024 | tf_op jit(solution)/shard_map/psum | solution.py:19
  278.0 0.0 copy-done.2
  278.1 2.0 multiply_reduce_fusion
  280.1 12.5 %psum.22 = f32[128]{0:T(128)S(1)} all-reduce(f32[128]{0:T(128)S(1)} %get-tuple-element.7), channel_id=1, replica_groups=mesh['grp'=8,'tp'=16] {'grp'}, use_global_device_ids=true, to_apply=%region_5.6 | all-reduce | flops 128 | bytes 1024 | tf_op jit(solution)/shard_map/psum | solution.py:24
  292.5 2.0 fusion.6
  294.6 0.0 all-gather.2.cloned.1.call-update
  295.3 80.7 %psum.23 = f32[]{:T(128)} all-reduce(f32[]{:T(128)S(6)} %mul_shard_map.3), channel_id=1, replica_groups=mesh['grp'=8,'tp'=16] {'grp','tp'}, use_global_device_ids=true, to_apply=%region_7.8 | all-reduce | flops 1 | bytes 8 | tf_op jit(solution)/shard_map/psum | solution.py:50
  376.0 0.0 all-gather.2.cloned.1.call-done
  376.0 18.6 %convert_bitcast_fusion = bf16[3072,1024]{0,1:T(8,128)(2,1)} fusion(bf16[2048,1024]{1,0:T(8,128)(2,1)} %all-gather.2.cloned.1.call-done, bf16[2048,3072]{1,0:T(8,128)(2,1)} %bitcast.10), kind=kOutput, calls=%fused_computation.1 | convolution fusion | flops 12888047616 | bytes 23068672 | tf_op jit(solution)/shard_map/dot_general | solution.py:51
  394.6 8.6 %copy.8 = bf16[3072,1024]{1,0:T(8,128)(2,1)} copy(bf16[3072,1024]{0,1:T(8,128)(2,1)} %convert_bitcast_fusion) | data formatting | bytes 12582912
  (4 shorter events, 0.0 us)
Async XLA Ops:
  7.2 254.4 %reduce-scatter.2.cloned.1.call-start = ((), (), s32[]{:S(2)}) async-start(), calls=%async_computation.2 | async-start | bytes 4456448 | tf_op jit(solution)/shard_map/reduce_scatter | solution.py:40
  14.8 151.0 %copy-start.3 = (bf16[3072,1024]{1,0:T(8,128)(2,1)S(1)}, bf16[3072,1024]{1,0:T(8,128)(2,1)}, u32[]{:S(2)}) copy-start(bf16[3072,1024]{1,0:T(8,128)(2,1)} %param.6) | copy-start | bytes 18874372
  161.2 4.6 %copy-start.1 = (bf16[8,256,3072]{2,1,0:T(8,128)(2,1)}, bf16[8,256,3072]{2,1,0:T(8,128)(2,1)S(1)}, u32[]{:S(2)}) copy-start(bf16[8,256,3072]{2,1,0:T(8,128)(2,1)S(1)} %all_to_all.5) | copy-start | bytes 37748740
  165.8 14.8 %copy-start = (s32[256]{0:T(256)S(1)}, s32[256]{0:T(256)}, u32[]{:S(2)}) copy-start(s32[256]{0:T(256)} %param.9) | copy-start | bytes 3076
  165.8 112.3 %copy-start.2 = (f32[1024]{0:T(1024)S(1)}, f32[1024]{0:T(1024)}, u32[]{:S(2)}) copy-start(f32[1024]{0:T(1024)} %param.7) | copy-start | bytes 12292
  180.6 195.4 %all-gather.2.cloned.1.call-start = ((), (), s32[]{:S(2)}) async-start(), calls=%async_computation.3 | async-start | bytes 4456448 | tf_op jit(solution)/shard_map/all_gather | solution.py:49
Sparse Core Ops, SparseCore 0:
  180.7 80.8 reduce-scatter.1
  294.7 62.8 all-gather.1
